TPU v7x, 32 devices: a whole 2x2x4 slice. The times are simulated.
32 devices in a mesh: grp: 4 (over x, core), row: 4 (over z), col: 2 (over y).
Axes of the slice: x: 2, y: 2, z: 4, core: 2. Of those that a mesh axis runs over, the one named last changes fastest.
Arguments:
- low_t: float32 [4, 4096, 768], P('grp', ('row', 'col')), may hold values from -8 to 8, as said below
- inv_first: float32 [4, 4096, 4096], P('grp', ('row', 'col')), may hold values from -8 to 8, as said below
- coupling_num: int32 [4, 4096, 4096], P('grp', ('row', 'col')), may hold values from -16 to 16
Outputs:
- solved: float32 [4, 4096, 768], P('grp', ('row', 'col'))
- swapped: float32 [4, 4096, 768], P('grp', ('row', 'col'))
Inputs may be any that keep to these rules, and one draw needn't show every extreme that they name: low_t[g, k, i] is zero where k > 3328 + i (rows of a lower-triangular matrix); its entries at k = 3328 + i lie in 0.5 to 2. inv_first[g] is lower triangular with diagonal entries in 0.5 to 2.
All inputs are finite; a program needn't handle non-finite values.
Results may differ from a plain program's by a relative error of at most 0.000071.
Values sent between devices are 32-bit elements; how exact they have to be, the bound alone decides.
A program may use at most 128 MiB of HBM per device.

v0:
```python
import functools
import jax
import jax.numpy as jnp
from jax import lax
from jax.experimental import pallas as pl
from jax.experimental.pallas import tpu as pltpu
from jax.sharding import PartitionSpec as P

B = 4096
BAND = 6144
CHUNKS = 16
LAGS = (0, 1, 2)
MESH = pl.DeviceIdType.MESH


def loop(count, body):
    def step(i, carry):
        body(i)
        return carry

    lax.fori_loop(0, count, step, 0)


def halves(value):
    high = value.astype(jnp.bfloat16)
    return high, (value - high.astype(jnp.float32)).astype(jnp.bfloat16)


def kernel(
    rows, cols, low_ref, inv_ref, num_ref, out_ref, swap_ref,
    num_tile, inv_tile, coupling, inv_high, inv_low, lhs, acc,
    sendb, own, col_in, row_in, hop_in,
    num_sem, inv_sem, col_send, col_recv, row_send, row_recv, hop_send, hop_recv, swap_send, swap_recv,
):
    chunks, width, block = low_ref.shape
    _, tall, total = inv_tile.shape
    tiles = block // tall
    sub = min(16, tall)
    r, c, g = lax.axis_index("row"), lax.axis_index("col"), lax.axis_index("grp")
    group = cols * block
    mate = g + 1 - 2 * lax.rem(g, 2)

    def needed(step, source, target):
        if step == 0:
            return total + source * group - (target + 1) * group + 1 <= BAND
        return target <= source

    barrier = pltpu.get_barrier_semaphore()
    peers = [{"grp": mate}]
    peers += [{"col": lax.rem(c + d, cols)} for d in range(1, cols)]
    peers += [{"row": lax.rem(r + d, rows)} for d in range(1, rows)]
    for peer in peers:
        pl.semaphore_signal(barrier, inc=1, device_id=peer, device_id_type=MESH)

    def num_copy(q):
        return pltpu.make_async_copy(
            num_ref.at[:, pl.ds(pl.multiple_of(q * block, block), block)], num_tile.at[q], num_sem.at[q]
        )

    def inv_copy(i):
        slot = lax.rem(i, 2)
        return pltpu.make_async_copy(
            inv_ref.at[pl.ds(pl.multiple_of(i * tall, tall), tall)], inv_tile.at[slot], inv_sem.at[slot]
        )

    def fetch(d):
        def column(z):
            @pl.when(needed(0, r, z))
            def _():
                num_copy(z * cols + lax.rem(c + d, cols)).start()

        loop(rows, column)

    for d in list(range(1, cols)) + [0]:
        fetch(d)
    inv_copy(0).start()

    def convert_num(q):
        num_copy(q).wait()
        high = min(64, block)

        def part(s):
            at = pl.ds(pl.multiple_of(s * high, high), high)
            row = (r * cols + c) * block + s * high + lax.broadcasted_iota(jnp.int32, (high, block), 0)
            col = q * block + lax.broadcasted_iota(jnp.int32, (high, block), 1)
            value = num_tile[q, at, :].astype(jnp.float32) * (1.0 / 64.0)
            value = jnp.where(total + row - col <= BAND, value, 0.0)
            coupling[at, pl.ds(pl.multiple_of(q * block, block), block)] = value.astype(jnp.bfloat16)

        loop(block // high, part)

    def convert_inv(i):
        @pl.when(i + 1 < tiles)
        def _():
            inv_copy(i + 1).start()

        inv_copy(i).wait()
        slot = lax.rem(i, 2)

        def part(s):
            at = pl.ds(pl.multiple_of(s * sub, sub), sub)
            to = pl.ds(pl.multiple_of(i * tall + s * sub, sub), sub)
            high, low = halves(inv_tile[slot, at, :])
            inv_high[to, :] = high
            inv_low[to, :] = low

        loop(tall // sub, part)

    def col_copy(step, n, d, z):
        return pltpu.make_async_remote_copy(
            src_ref=sendb.at[n, d - 1, z],
            dst_ref=col_in.at[step, n, d - 1, z],
            send_sem=col_send.at[step, n, d - 1, z],
            recv_sem=col_recv.at[step, n, d - 1, z],
            device_id={"col": lax.rem(c + d, cols)},
            device_id_type=MESH,
        )

    def row_copy(n, d):
        target = lax.rem(r + d, rows)
        return pltpu.make_async_remote_copy(
            src_ref=own.at[n, target],
            dst_ref=row_in.at[n, d - 1],
            send_sem=row_send.at[n, d - 1],
            recv_sem=row_recv.at[n, d - 1],
            device_id={"row": target},
            device_id_type=MESH,
        )

    def hop_copy(n, slot, source):
        return pltpu.make_async_remote_copy(
            src_ref=source,
            dst_ref=hop_in.at[n, slot],
            send_sem=hop_send.at[n, slot],
            recv_sem=hop_recv.at[n, slot],
            device_id={"row": lax.rem(r + rows - 1, rows)},
            device_id_type=MESH,
        )

    def far_copy(n, d):
        return hop_copy(n, rows - 2 + d, sendb.at[n, d - 1, 0])

    def near_copy(n, z):
        return hop_copy(n, z, own.at[n, z])

    def swap_copy(n):
        return pltpu.make_async_remote_copy(
            src_ref=out_ref.at[n],
            dst_ref=swap_ref.at[n],
            send_sem=swap_send.at[n],
            recv_sem=swap_recv.at[n],
            device_id={"grp": mate},
            device_id_type=MESH,
        )

    def term(step, owner):
        at = pl.ds(pl.multiple_of(owner * block, block), block)
        right = coupling if step == 0 else inv_high
        both = jnp.dot(lhs[...], right[:, at], preferred_element_type=jnp.float32)
        result = both[:width] + both[width:]
        if step == 1:
            result += jnp.dot(lhs[:width], inv_low[:, at], preferred_element_type=jnp.float32)
        return result

    def form(step, n, value):
        high, low = halves(value)
        lhs[:width] = high
        lhs[width:] = low

        def ready(q):
            if step == 0:
                @pl.when(n == 0)
                def _():
                    convert_num(q)

        def away(z):
            @pl.when((z < rows) & needed(step, r, z))
            def _():
                for d in range(1, cols):
                    owner = z * cols + lax.rem(c + d, cols)
                    ready(owner)
                    sendb[n, d - 1, z] = term(step, owner)

            @pl.when((z > step) & needed(step, r, z - 1))
            def _():
                for d in range(1, cols):
                    col_copy(step, n, d, z - 1).start()

        def home(z):
            @pl.when(needed(step, r, z))
            def _():
                ready(z * cols + c)
                own[n, z] = term(step, z * cols + c)

        loop(rows + 1, away)
        loop(rows, home)

    def join(n):
        def add(z):
            @pl.when(needed(0, r, z))
            def _():
                for d in range(1, cols):
                    col_copy(0, n, d, z).wait_recv()
                    own[n, z] += col_in[0, n, d - 1, z]

        loop(rows, add)
        for d in range(1, rows):
            @pl.when(needed(0, r, lax.rem(r + d, rows)))
            def _():
                row_copy(n, d).start()

    def middle(n):
        acc[...] = own[n, r]
        for d in range(1, rows):
            @pl.when(needed(0, lax.rem(r + rows - d, rows), r))
            def _():
                row_copy(n, d).wait_recv()
                acc[...] += row_in[n, d - 1]
        for d in range(1, rows):
            @pl.when(needed(0, r, lax.rem(r + d, rows)))
            def _():
                row_copy(n, d).wait_send()

        def sent(z):
            @pl.when(needed(0, r, z))
            def _():
                for d in range(1, cols):
                    col_copy(0, n, d, z).wait_send()

        loop(rows, sent)
        form(1, n, acc[...])

    above, below = r < rows - 1, r > 0

    def relay(n):
        @pl.when(above)
        def _():
            near_copy(n, 0).wait_recv()
            own[n, 0] += hop_in[n, 0]
            for d in range(1, cols):
                far_copy(n, d).wait_recv()
                sendb[n, d - 1, 0] += hop_in[n, rows - 2 + d]

        @pl.when(below)
        def _():
            near_copy(n, 0).start()
            for d in range(1, cols):
                far_copy(n, d).start()

        @pl.when(r == 0)
        def _():
            for d in range(1, cols):
                col_copy(1, n, d, 0).start()

        for z in range(1, rows):
            @pl.when(z <= r)
            def _():
                for d in range(1, cols):
                    col_copy(1, n, d, z).wait_recv()
                    own[n, z] += col_in[1, n, d - 1, z]

            if z < rows - 1:
                @pl.when((z <= r) & above)
                def _():
                    near_copy(n, z).wait_recv()
                    own[n, z] += hop_in[n, z]

                @pl.when(z < r)
                def _():
                    near_copy(n, z).start()

    def last(n):
        @pl.when(r == 0)
        def _():
            for d in range(1, cols):
                col_copy(1, n, d, 0).wait_recv()
                own[n, 0] += col_in[1, n, d - 1, 0]

        out_ref[n] = -own[n, r]
        swap_copy(n).start()

    def settle(n):
        for d in range(1, cols):
            @pl.when(r == 0)
            def _():
                col_copy(1, n, d, 0).wait_send()

            @pl.when(below)
            def _():
                far_copy(n, d).wait_send()

        for z in range(rows):
            if z > 0:
                @pl.when(z <= r)
                def _():
                    for d in range(1, cols):
                        col_copy(1, n, d, z).wait_send()

            if z < rows - 1:
                @pl.when(z < r)
                def _():
                    near_copy(n, z).wait_send()

        swap_copy(n).wait()

    pl.semaphore_wait(barrier, len(peers))

    def stage(t, lag, body):
        n = t - lag

        @pl.when((n >= 0) & (n < chunks))
        def _():
            body(n)

    def pipeline(t):
        stage(t, LAGS[0], lambda n: form(0, n, low_ref[n]))

        stage(t, LAGS[1], join)

        @pl.when(t == LAGS[1])
        def _():
            loop(tiles, convert_inv)

        stage(t, LAGS[2], middle)
        lag = LAGS[2] + rows - r
        stage(t, lag, relay)
        stage(t, lag + jnp.where(r == 0, 1, 0), last)

    loop(chunks + LAGS[2] + rows + 1, pipeline)
    loop(chunks, settle)


def local(low_t, inv_first, coupling_num):
    rows, cols = lax.axis_size("row"), lax.axis_size("col")
    _, block, width = low_t.shape
    total = inv_first.shape[2]
    chunk = width // CHUNKS
    low = low_t[0].T.reshape(CHUNKS, chunk, block)
    tiles = 8
    tall = block // tiles
    vmem = functools.partial(pl.BlockSpec, memory_space=pltpu.VMEM)
    hbm = functools.partial(pl.BlockSpec, memory_space=pl.ANY)
    dma = pltpu.SemaphoreType.DMA
    piece = (chunk, block)
    hops = rows + cols - 2
    result = jax.ShapeDtypeStruct((CHUNKS,) + piece, jnp.float32)
    solved, swapped = pl.pallas_call(
        functools.partial(kernel, rows, cols),
        out_shape=(result, result),
        in_specs=[vmem(), hbm(), hbm()],
        out_specs=(vmem(), hbm()),
        scratch_shapes=[
            pltpu.VMEM((rows * cols, block, block), jnp.int32),
            pltpu.VMEM((2, tall, total), jnp.float32),
            pltpu.VMEM((block, total), jnp.bfloat16),
            pltpu.VMEM((block, total), jnp.bfloat16),
            pltpu.VMEM((block, total), jnp.bfloat16),
            pltpu.VMEM((2 * chunk, block), jnp.bfloat16),
            pltpu.VMEM(piece, jnp.float32),
            pltpu.VMEM((CHUNKS, cols - 1, rows) + piece, jnp.float32),
            pltpu.VMEM((CHUNKS, rows) + piece, jnp.float32),
            pltpu.VMEM((2, CHUNKS, cols - 1, rows) + piece, jnp.float32),
            pltpu.VMEM((CHUNKS, rows - 1) + piece, jnp.float32),
            pltpu.VMEM((CHUNKS, hops) + piece, jnp.float32),
            dma((rows * cols,)),
            dma((2,)),
            dma((2, CHUNKS, cols - 1, rows)),
            dma((2, CHUNKS, cols - 1, rows)),
            dma((CHUNKS, rows - 1)),
            dma((CHUNKS, rows - 1)),
            dma((CHUNKS, hops)),
            dma((CHUNKS, hops)),
            dma((CHUNKS,)),
            dma((CHUNKS,)),
        ],
        compiler_params=pltpu.CompilerParams(
            collective_id=0, has_side_effects=True, vmem_limit_bytes=67043328
        ),
    )(low, inv_first[0], coupling_num[0])
    return (
        solved.reshape(width, block).T[None],
        swapped.reshape(width, block).T[None],
    )


def solution(mesh):
    placed = (
        P("grp", ("row", "col"), None),
        P("grp", ("row", "col"), None),
        P("grp", ("row", "col"), None),
    )
    return jax.shard_map(
        local,
        mesh=mesh,
        in_specs=placed,
        out_specs=(P("grp", ("row", "col"), None), P("grp", ("row", "col"), None)),
        check_vma=False,
    )
```

profile of v0, /device:TPU:0, one launch (start us, length us, event | category | flops | bytes accessed | tf_op | source)
XLA Modules:
  0.0 253.1 jit_solution(2581629823650102753)
XLA Ops:
  0.6 3.0 %copy.5 = f32[768,512]{1,0:T(8,128)} copy(f32[768,512]{0,1:T(8,128)} %bitcast.17) | data formatting | bytes 3145728 | tf_op jit(solution)/shard_map/transpose | solution.py:338
  3.7 244.7 %shard_map.50 = (f32[16,48,512]{2,1,0:T(8,128)}, f32[16,48,512]{2,1,0:T(8,128)}) custom-call(f32[16,48,512]{2,1,0:T(8,128)} %bitcast.16, f32[512,4096]{1,0:T(8,128)} %bitcast.14, s32[512,4096]{1,0:T(8,128)} %bitcast.15), custom_call_target="tpu_custom_call" | custom-call | tf_op jit(solution)/shard_map/pallas_call | solution.py:347
  248.3 0.0 copy-start
  248.4 3.1 %copy.6 = f32[768,512]{0,1:T(8,128)} copy(f32[768,512]{1,0:T(8,128)} %bitcast.21) | data formatting | bytes 3145728 | tf_op jit(solution)/shard_map/reshape | solution.py:381
  251.5 0.0 copy-done
  251.5 1.6 copy.7
Async XLA Ops:
  248.3 3.2 %copy-start = (f32[16,48,512]{2,1,0:T(8,128)S(1)}, f32[16,48,512]{2,1,0:T(8,128)}, u32[]{:S(2)}) copy-start(f32[16,48,512]{2,1,0:T(8,128)} %get-tuple-element.5) | copy-start | bytes 4718596
where the time goes:
time: 253 us
  Pallas kernels  245 us (97%)
  local copies, waits for them, and re-layouts  7.78 us (3%)
    pallas_call x1, Pallas kernels, local(): pl.pallas_call(functools.partial(kernel, rows, cols), out_shape=(result,...  245 us

commit v1 on v0

--- a/solution.py
+++ b/solution.py
@@ -8,8 +8,10 @@
 
 B = 4096
 BAND = 6144
-CHUNKS = 16
-LAGS = (0, 1, 2)
+CHUNKS = 24
+LAGS = (0, 1, 3)
+SPLIT = 10
+READY = 2
 MESH = pl.DeviceIdType.MESH
 
 
@@ -28,11 +30,14 @@
 
 def kernel(
     rows, cols, low_ref, inv_ref, num_ref, out_ref, swap_ref,
-    num_tile, inv_tile, coupling, inv_high, inv_low, lhs, acc,
-    sendb, own, col_in, row_in, hop_in,
-    num_sem, inv_sem, col_send, col_recv, row_send, row_recv, hop_send, hop_recv, swap_send, swap_recv,
+    num_tile, inv_tile, coupling, inv_high, inv_low, turned, lhs, acc,
+    sendb, own, col_in, row_in, hub_in, hop_in,
+    num_sem, inv_sem, col_send, col_recv, row_send, row_recv, hub_send, hub_recv,
+    hop_send, hop_recv, swap_send, swap_recv,
 ):
-    chunks, width, block = low_ref.shape
+    chunks, width = own.shape[0], own.shape[2]
+    block = low_ref.shape[0]
+    group_of = turned.shape[0] // width
     _, tall, total = inv_tile.shape
     tiles = block // tall
     sub = min(16, tall)
@@ -44,6 +49,21 @@
         if step == 0:
             return total + source * group - (target + 1) * group + 1 <= BAND
         return target <= source
+
+    final, hub = rows - 1, rows - 2
+
+    def crosses(step, n, source, z, target):
+        q, p = r * cols + source, z * cols + target
+        if step == 0:
+            inside = total + (q - p - 1) * block + 1 <= BAND
+            return inside & (q * block < total - (chunks - n - 1) * width)
+        return p <= q
+
+    def pooled(source, target):
+        return (source == final) & (target < hub) & needed(0, source, target)
+
+    def direct(n):
+        return (r == final) & (final > 0) & (n >= SPLIT)
 
     barrier = pltpu.get_barrier_semaphore()
     peers = [{"grp": mate}]
@@ -127,6 +147,16 @@
             device_id_type=MESH,
         )
 
+    def hub_copy(n, z):
+        return pltpu.make_async_remote_copy(
+            src_ref=own.at[n, z],
+            dst_ref=hub_in.at[n, z],
+            send_sem=hub_send.at[n, z],
+            recv_sem=hub_recv.at[n, z],
+            device_id={"row": lax.rem(r + rows - 1, rows)},
+            device_id_type=MESH,
+        )
+
     def hop_copy(n, slot, source):
         return pltpu.make_async_remote_copy(
             src_ref=source,
@@ -143,12 +173,15 @@
     def near_copy(n, z):
         return hop_copy(n, z, own.at[n, z])
 
-    def swap_copy(n):
+    def lanes(b):
+        return pl.ds(pl.multiple_of(b * turned.shape[0], turned.shape[0]), turned.shape[0])
+
+    def swap_copy(b):
         return pltpu.make_async_remote_copy(
-            src_ref=out_ref.at[n],
-            dst_ref=swap_ref.at[n],
-            send_sem=swap_send.at[n],
-            recv_sem=swap_recv.at[n],
+            src_ref=out_ref.at[:, lanes(b)],
+            dst_ref=swap_ref.at[:, lanes(b)],
+            send_sem=swap_send.at[b],
+            recv_sem=swap_recv.at[b],
             device_id={"grp": mate},
             device_id_type=MESH,
         )
@@ -173,20 +206,42 @@
                 def _():
                     convert_num(q)
 
-        def away(z):
-            @pl.when((z < rows) & needed(step, r, z))
+        def wanted(z, d):
+            target = lax.rem(c + d, cols)
+            if step == 0:
+                return crosses(0, n, c, z, target)
+            return (z == 0) | crosses(1, n, c, z, target)
+
+        def turn(i):
+            return rows - 1 - i if step == 0 else i
+
+        def away(i):
+            z, before = turn(i), turn(i - 1)
+
+            @pl.when((i < rows) & needed(step, r, z))
             def _():
                 for d in range(1, cols):
                     owner = z * cols + lax.rem(c + d, cols)
                     ready(owner)
-                    sendb[n, d - 1, z] = term(step, owner)
-
-            @pl.when((z > step) & needed(step, r, z - 1))
+
+                    @pl.when(wanted(z, d))
+                    def _():
+                        sendb[n, d - 1, z] = term(step, owner)
+
+            @pl.when((i > 0) & needed(step, r, before))
             def _():
                 for d in range(1, cols):
-                    col_copy(step, n, d, z - 1).start()
-
-        def home(z):
+                    go = wanted(before, d)
+                    if step == 1:
+                        go = go & ((before > 0) | direct(n))
+
+                    @pl.when(go)
+                    def _():
+                        col_copy(step, n, d, before).start()
+
+        def home(i):
+            z = turn(i)
+
             @pl.when(needed(step, r, z))
             def _():
                 ready(z * cols + c)
@@ -194,49 +249,93 @@
 
         loop(rows + 1, away)
         loop(rows, home)
+
+    def held(target):
+        return (r == hub) & pooled(final, target)
 
     def join(n):
         def add(z):
             @pl.when(needed(0, r, z))
             def _():
                 for d in range(1, cols):
-                    col_copy(0, n, d, z).wait_recv()
-                    own[n, z] += col_in[0, n, d - 1, z]
+                    @pl.when(crosses(0, n, lax.rem(c + cols - d, cols), z, c))
+                    def _():
+                        col_copy(0, n, d, z).wait_recv()
+                        own[n, z] += col_in[0, n, d - 1, z]
 
         loop(rows, add)
-        for d in range(1, rows):
-            @pl.when(needed(0, r, lax.rem(r + d, rows)))
-            def _():
-                row_copy(n, d).start()
+        for target in reversed(range(rows)):
+            @pl.when((target != r) & needed(0, r, target) & ~pooled(r, target) & ~held(target))
+            def _():
+                row_copy(n, lax.rem(target - r + rows, rows)).start()
+
+        for z in range(hub):
+            @pl.when(pooled(r, z))
+            def _():
+                hub_copy(n, z).start()
+
+    def pool(n):
+        for z in range(hub):
+            @pl.when(held(z))
+            def _():
+                hub_copy(n, z).wait_recv()
+                own[n, z] += hub_in[n, z]
+
+        for z in range(hub):
+            @pl.when(held(z))
+            def _():
+                row_copy(n, z - hub + rows).start()
 
     def middle(n):
         acc[...] = own[n, r]
         for d in range(1, rows):
-            @pl.when(needed(0, lax.rem(r + rows - d, rows), r))
+            source = lax.rem(r + rows - d, rows)
+
+            @pl.when(needed(0, source, r) & ~pooled(source, r))
             def _():
                 row_copy(n, d).wait_recv()
                 acc[...] += row_in[n, d - 1]
         for d in range(1, rows):
-            @pl.when(needed(0, r, lax.rem(r + d, rows)))
+            target = lax.rem(r + d, rows)
+
+            @pl.when(needed(0, r, target) & ~pooled(r, target))
             def _():
                 row_copy(n, d).wait_send()
+        for z in range(hub):
+            @pl.when(pooled(r, z))
+            def _():
+                hub_copy(n, z).wait_send()
 
         def sent(z):
             @pl.when(needed(0, r, z))
             def _():
                 for d in range(1, cols):
-                    col_copy(0, n, d, z).wait_send()
+                    @pl.when(crosses(0, n, c, z, lax.rem(c + d, cols)))
+                    def _():
+                        col_copy(0, n, d, z).wait_send()
 
         loop(rows, sent)
         form(1, n, acc[...])
 
-    above, below = r < rows - 1, r > 0
+    above, below = r < final, r > 0
+
+    def spread(n):
+        return ~((r + 1 == final) & (n >= SPLIT))
 
     def relay(n):
+        @pl.when(direct(n))
+        def _():
+            for d in range(1, cols):
+                col_copy(1, n, d, 0).wait_recv()
+                own[n, 0] += col_in[1, n, d - 1, 0]
+
         @pl.when(above)
         def _():
             near_copy(n, 0).wait_recv()
             own[n, 0] += hop_in[n, 0]
+
+        @pl.when(above & spread(n))
+        def _():
             for d in range(1, cols):
                 far_copy(n, d).wait_recv()
                 sendb[n, d - 1, 0] += hop_in[n, rows - 2 + d]
@@ -244,6 +343,9 @@
         @pl.when(below)
         def _():
             near_copy(n, 0).start()
+
+        @pl.when(below & ~direct(n))
+        def _():
             for d in range(1, cols):
                 far_copy(n, d).start()
 
@@ -256,8 +358,10 @@
             @pl.when(z <= r)
             def _():
                 for d in range(1, cols):
-                    col_copy(1, n, d, z).wait_recv()
-                    own[n, z] += col_in[1, n, d - 1, z]
+                    @pl.when(crosses(1, n, lax.rem(c + cols - d, cols), z, c))
+                    def _():
+                        col_copy(1, n, d, z).wait_recv()
+                        own[n, z] += col_in[1, n, d - 1, z]
 
             if z < rows - 1:
                 @pl.when((z <= r) & above)
@@ -276,24 +380,28 @@
                 col_copy(1, n, d, 0).wait_recv()
                 own[n, 0] += col_in[1, n, d - 1, 0]
 
-        out_ref[n] = -own[n, r]
-        swap_copy(n).start()
+        @pl.when(lax.rem(n, group_of) == group_of - 1)
+        def _():
+            b = lax.div(n, group_of)
+            piece = own[pl.ds(n - (group_of - 1), group_of), r]
+            out_ref[:, lanes(b)] = -piece.reshape(group_of * width, block).T
+            swap_copy(b).start()
 
     def settle(n):
         for d in range(1, cols):
-            @pl.when(r == 0)
+            @pl.when((r == 0) | direct(n))
             def _():
                 col_copy(1, n, d, 0).wait_send()
 
-            @pl.when(below)
+            @pl.when(below & ~direct(n))
             def _():
                 far_copy(n, d).wait_send()
 
         for z in range(rows):
             if z > 0:
-                @pl.when(z <= r)
-                def _():
-                    for d in range(1, cols):
+                for d in range(1, cols):
+                    @pl.when((z <= r) & crosses(1, n, c, z, lax.rem(c + d, cols)))
+                    def _():
                         col_copy(1, n, d, z).wait_send()
 
             if z < rows - 1:
@@ -301,7 +409,9 @@
                 def _():
                     near_copy(n, z).wait_send()
 
-        swap_copy(n).wait()
+        @pl.when(lax.rem(n, group_of) == 0)
+        def _():
+            swap_copy(lax.div(n, group_of)).wait()
 
     pl.semaphore_wait(barrier, len(peers))
 
@@ -313,15 +423,31 @@
             body(n)
 
     def pipeline(t):
-        stage(t, LAGS[0], lambda n: form(0, n, low_ref[n]))
+        @pl.when((t < chunks) & (lax.rem(t, group_of) == 0))
+        def _():
+            turned[...] = low_ref[:, lanes(lax.div(t, group_of))].T
+
+        def head(n):
+            at = pl.multiple_of(lax.rem(n, group_of) * width, width)
+            form(0, n, turned[pl.ds(at, width)])
+
+        stage(t, LAGS[0], head)
 
         stage(t, LAGS[1], join)
 
-        @pl.when(t == LAGS[1])
+        @pl.when(t == READY)
         def _():
             loop(tiles, convert_inv)
 
-        stage(t, LAGS[2], middle)
+        if hub > 0:
+            @pl.when((r == hub) & pooled(final, hub - 1))
+            def _():
+                stage(t, LAGS[2], pool)
+
+            late = (r <= hub) & pooled(final, jnp.minimum(r, hub - 1))
+            stage(t, LAGS[2] + jnp.where(late, 1, 0), middle)
+        else:
+            stage(t, LAGS[2], middle)
         lag = LAGS[2] + rows - r
         stage(t, lag, relay)
         stage(t, lag + jnp.where(r == 0, 1, 0), last)
@@ -335,7 +461,7 @@
     _, block, width = low_t.shape
     total = inv_first.shape[2]
     chunk = width // CHUNKS
-    low = low_t[0].T.reshape(CHUNKS, chunk, block)
+    turn = 128
     tiles = 8
     tall = block // tiles
     vmem = functools.partial(pl.BlockSpec, memory_space=pltpu.VMEM)
@@ -343,7 +469,7 @@
     dma = pltpu.SemaphoreType.DMA
     piece = (chunk, block)
     hops = rows + cols - 2
-    result = jax.ShapeDtypeStruct((CHUNKS,) + piece, jnp.float32)
+    result = jax.ShapeDtypeStruct((block, width), jnp.float32)
     solved, swapped = pl.pallas_call(
         functools.partial(kernel, rows, cols),
         out_shape=(result, result),
@@ -355,12 +481,14 @@
             pltpu.VMEM((block, total), jnp.bfloat16),
             pltpu.VMEM((block, total), jnp.bfloat16),
             pltpu.VMEM((block, total), jnp.bfloat16),
+            pltpu.VMEM((turn, block), jnp.float32),
             pltpu.VMEM((2 * chunk, block), jnp.bfloat16),
             pltpu.VMEM(piece, jnp.float32),
             pltpu.VMEM((CHUNKS, cols - 1, rows) + piece, jnp.float32),
             pltpu.VMEM((CHUNKS, rows) + piece, jnp.float32),
             pltpu.VMEM((2, CHUNKS, cols - 1, rows) + piece, jnp.float32),
             pltpu.VMEM((CHUNKS, rows - 1) + piece, jnp.float32),
+            pltpu.VMEM((CHUNKS, rows - 2) + piece, jnp.float32),
             pltpu.VMEM((CHUNKS, hops) + piece, jnp.float32),
             dma((rows * cols,)),
             dma((2,)),
@@ -368,19 +496,18 @@
             dma((2, CHUNKS, cols - 1, rows)),
             dma((CHUNKS, rows - 1)),
             dma((CHUNKS, rows - 1)),
+            dma((CHUNKS, rows - 2)),
+            dma((CHUNKS, rows - 2)),
             dma((CHUNKS, hops)),
             dma((CHUNKS, hops)),
-            dma((CHUNKS,)),
-            dma((CHUNKS,)),
+            dma((width // turn,)),
+            dma((width // turn,)),
         ],
         compiler_params=pltpu.CompilerParams(
             collective_id=0, has_side_effects=True, vmem_limit_bytes=67043328
         ),
-    )(low, inv_first[0], coupling_num[0])
-    return (
-        solved.reshape(width, block).T[None],
-        swapped.reshape(width, block).T[None],
-    )
+    )(low_t[0], inv_first[0], coupling_num[0])
+    return solved[None], swapped[None]
 
 
 def solution(mesh):

time: 253 us -> 230 us (0.909)
  Pallas kernels: 245 us -> 225 us
  local copies, waits for them, and re-layouts: 7.78 us -> 3.92 us
    pallas_call x1, Pallas kernels: 245 us -> 225 us  [local(): pl.pallas_call(functools.partial(kernel, rows, cols), out_shape=(result,...]
    reshape x2 -> x0, local copies, waits for them, and re-layouts: 4.75 us -> none  [the longest x1 3.14 us: local(): solved.reshape(width, block).T[None]]
    unnamed x2 -> x4, local copies, waits for them, and re-layouts: 0.01 us -> 3.92 us
    transpose x1 -> x0, local copies, waits for them, and re-layouts: 3.02 us -> none  [local(): low = low_t[0].T.reshape(CHUNKS, chunk, block)]
where the time goes in v1:
time: 230 us
  Pallas kernels  225 us (98%)
  local copies, waits for them, and re-layouts  3.92 us (2%)
    pallas_call x1, Pallas kernels, local(): pl.pallas_call(functools.partial(kernel, rows, cols), out_shape=(result,...  225 us

profile of v1, /device:TPU:0, one launch (start us, length us, event | category | flops | bytes accessed | tf_op | source)
XLA Modules:
  0.0 229.7 jit_solution(11214536643841493050)
XLA Ops:
  0.6 225.1 %shard_map.50 = (f32[512,768]{1,0:T(8,128)}, f32[512,768]{1,0:T(8,128)}) custom-call(f32[512,768]{1,0:T(8,128)} %bitcast.7, f32[512,4096]{1,0:T(8,128)} %bitcast.5, s32[512,4096]{1,0:T(8,128)} %bitcast.6), custom_call_target="tpu_custom_call" | custom-call | tf_op jit(solution)/shard_map/pallas_call | solution.py:473
  225.8 0.0 copy-start
  225.8 2.8 %copy.7 = f32[1,512,768]{2,1,0:T(8,128)} copy(f32[1,512,768]{2,1,0:T(8,128)} %bitcast.9) | data formatting | bytes 3145728
  228.5 0.0 copy-done
  228.5 1.1 copy.8
Async XLA Ops:
  225.8 2.8 %copy-start = (f32[512,768]{1,0:T(8,128)S(1)}, f32[512,768]{1,0:T(8,128)}, u32[]{:S(2)}) copy-start(f32[512,768]{1,0:T(8,128)} %get-tuple-element.5) | copy-start | bytes 4718596

commit v2 on v1

--- a/solution.py
+++ b/solution.py
@@ -12,6 +12,7 @@
 LAGS = (0, 1, 3)
 SPLIT = 10
 READY = 2
+PAUSE = 3
 MESH = pl.DeviceIdType.MESH
 
 
@@ -51,6 +52,7 @@
         return target <= source
 
     final, hub = rows - 1, rows - 2
+    cut = max(1, rows // 2)
 
     def crosses(step, n, source, z, target):
         q, p = r * cols + source, z * cols + target
@@ -126,15 +128,26 @@
 
         loop(tall // sub, part)
 
-    def col_copy(step, n, d, z):
+    def col_copy(step, n, d, z, count=1):
         return pltpu.make_async_remote_copy(
-            src_ref=sendb.at[n, d - 1, z],
-            dst_ref=col_in.at[step, n, d - 1, z],
+            src_ref=sendb.at[n, d - 1, pl.ds(z, count)],
+            dst_ref=col_in.at[step, n, d - 1, pl.ds(z, count)],
             send_sem=col_send.at[step, n, d - 1, z],
             recv_sem=col_recv.at[step, n, d - 1, z],
             device_id={"col": lax.rem(c + d, cols)},
             device_id_type=MESH,
         )
+
+    def span(step, n, d, sending, act, begin=0, end=rows):
+        source, target = (c, lax.rem(c + d, cols)) if sending else (lax.rem(c + cols - d, cols), c)
+        first = jnp.where(direct(n), 0, 1) if step == 1 and begin == 0 else begin
+        length = 0
+        for z in range(begin, end):
+            length = length + jnp.where(crosses(step, n, source, z, target) & (z >= first), 1, 0)
+        for count in range(1, end - begin + 1):
+            @pl.when(length == count)
+            def _():
+                act(col_copy(step, n, d, first if step == 1 else rows - count, count))
 
     def row_copy(n, d):
         target = lax.rem(r + d, rows)
@@ -195,7 +208,7 @@
             result += jnp.dot(lhs[:width], inv_low[:, at], preferred_element_type=jnp.float32)
         return result
 
-    def form(step, n, value):
+    def form(step, n, value, begin=0, end=rows):
         high, low = halves(value)
         lhs[:width] = high
         lhs[width:] = low
@@ -213,12 +226,12 @@
             return (z == 0) | crosses(1, n, c, z, target)
 
         def turn(i):
-            return rows - 1 - i if step == 0 else i
+            return rows - 1 - i if step == 0 else begin + i
 
         def away(i):
-            z, before = turn(i), turn(i - 1)
-
-            @pl.when((i < rows) & needed(step, r, z))
+            z = turn(i)
+
+            @pl.when(needed(step, r, z))
             def _():
                 for d in range(1, cols):
                     owner = z * cols + lax.rem(c + d, cols)
@@ -228,17 +241,6 @@
                     def _():
                         sendb[n, d - 1, z] = term(step, owner)
 
-            @pl.when((i > 0) & needed(step, r, before))
-            def _():
-                for d in range(1, cols):
-                    go = wanted(before, d)
-                    if step == 1:
-                        go = go & ((before > 0) | direct(n))
-
-                    @pl.when(go)
-                    def _():
-                        col_copy(step, n, d, before).start()
-
         def home(i):
             z = turn(i)
 
@@ -247,20 +249,26 @@
                 ready(z * cols + c)
                 own[n, z] = term(step, z * cols + c)
 
-        loop(rows + 1, away)
-        loop(rows, home)
+        loop(end - begin, away)
+        home(0)
+        for d in range(1, cols):
+            span(step, n, d, True, lambda copy: copy.start(), begin, end)
+        if end - begin > 1:
+            loop(end - begin - 1, lambda i: home(i + 1))
 
     def held(target):
         return (r == hub) & pooled(final, target)
 
     def join(n):
+        for d in range(1, cols):
+            span(0, n, d, False, lambda copy: copy.wait_recv())
+
         def add(z):
             @pl.when(needed(0, r, z))
             def _():
                 for d in range(1, cols):
                     @pl.when(crosses(0, n, lax.rem(c + cols - d, cols), z, c))
                     def _():
-                        col_copy(0, n, d, z).wait_recv()
                         own[n, z] += col_in[0, n, d - 1, z]
 
         loop(rows, add)
@@ -306,16 +314,13 @@
             def _():
                 hub_copy(n, z).wait_send()
 
-        def sent(z):
-            @pl.when(needed(0, r, z))
-            def _():
-                for d in range(1, cols):
-                    @pl.when(crosses(0, n, c, z, lax.rem(c + d, cols)))
-                    def _():
-                        col_copy(0, n, d, z).wait_send()
-
-        loop(rows, sent)
-        form(1, n, acc[...])
+        for d in range(1, cols):
+            span(0, n, d, True, lambda copy: copy.wait_send())
+        own[n, r] = acc[...]
+        form(1, n, acc[...], 0, cut)
+
+    def middle_rest(n):
+        form(1, n, own[n, r], cut, rows)
 
     above, below = r < final, r > 0
 
@@ -323,27 +328,12 @@
         return ~((r + 1 == final) & (n >= SPLIT))
 
     def relay(n):
-        @pl.when(direct(n))
-        def _():
-            for d in range(1, cols):
-                col_copy(1, n, d, 0).wait_recv()
-                own[n, 0] += col_in[1, n, d - 1, 0]
-
-        @pl.when(above)
-        def _():
-            near_copy(n, 0).wait_recv()
-            own[n, 0] += hop_in[n, 0]
-
         @pl.when(above & spread(n))
         def _():
             for d in range(1, cols):
                 far_copy(n, d).wait_recv()
                 sendb[n, d - 1, 0] += hop_in[n, rows - 2 + d]
 
-        @pl.when(below)
-        def _():
-            near_copy(n, 0).start()
-
         @pl.when(below & ~direct(n))
         def _():
             for d in range(1, cols):
@@ -354,13 +344,43 @@
             for d in range(1, cols):
                 col_copy(1, n, d, 0).start()
 
-        for z in range(1, rows):
+        def gather():
+            for d in range(1, cols):
+                span(1, n, d, False, lambda copy: copy.wait_recv(), 0, cut)
+
+        @pl.when(direct(n))
+        def _():
+            gather()
+            for d in range(1, cols):
+                own[n, 0] += col_in[1, n, d - 1, 0]
+
+        @pl.when(above)
+        def _():
+            near_copy(n, 0).wait_recv()
+            own[n, 0] += hop_in[n, 0]
+
+        @pl.when(below)
+        def _():
+            near_copy(n, 0).start()
+
+        @pl.when(~direct(n))
+        def _():
+            gather()
+
+        carry(n, 1, cut)
+
+    def relay_rest(n):
+        for d in range(1, cols):
+            span(1, n, d, False, lambda copy: copy.wait_recv(), cut, rows)
+        carry(n, cut, rows)
+
+    def carry(n, begin, end):
+        for z in range(begin, end):
             @pl.when(z <= r)
             def _():
                 for d in range(1, cols):
                     @pl.when(crosses(1, n, lax.rem(c + cols - d, cols), z, c))
                     def _():
-                        col_copy(1, n, d, z).wait_recv()
                         own[n, z] += col_in[1, n, d - 1, z]
 
             if z < rows - 1:
@@ -384,12 +404,16 @@
         def _():
             b = lax.div(n, group_of)
             piece = own[pl.ds(n - (group_of - 1), group_of), r]
-            out_ref[:, lanes(b)] = -piece.reshape(group_of * width, block).T
+            out_ref[:, lanes(b)] = piece.reshape(group_of * width, block).T
             swap_copy(b).start()
 
     def settle(n):
         for d in range(1, cols):
-            @pl.when((r == 0) | direct(n))
+            span(1, n, d, True, lambda copy: copy.wait_send(), 0, cut)
+            if cut < rows:
+                span(1, n, d, True, lambda copy: copy.wait_send(), cut, rows)
+
+            @pl.when(r == 0)
             def _():
                 col_copy(1, n, d, 0).wait_send()
 
@@ -398,12 +422,6 @@
                 far_copy(n, d).wait_send()
 
         for z in range(rows):
-            if z > 0:
-                for d in range(1, cols):
-                    @pl.when((z <= r) & crosses(1, n, c, z, lax.rem(c + d, cols)))
-                    def _():
-                        col_copy(1, n, d, z).wait_send()
-
             if z < rows - 1:
                 @pl.when(z < r)
                 def _():
@@ -439,20 +457,30 @@
         def _():
             loop(tiles, convert_inv)
 
+        late = 0
         if hub > 0:
             @pl.when((r == hub) & pooled(final, hub - 1))
             def _():
                 stage(t, LAGS[2], pool)
 
-            late = (r <= hub) & pooled(final, jnp.minimum(r, hub - 1))
-            stage(t, LAGS[2] + jnp.where(late, 1, 0), middle)
-        else:
-            stage(t, LAGS[2], middle)
+            late = jnp.where((r <= hub) & pooled(final, jnp.minimum(r, hub - 1)), 1, 0)
         lag = LAGS[2] + rows - r
+        rest = jnp.where(r >= cut, PAUSE, 0)
+        stage(t, LAGS[2] + late, middle)
+        if cut < rows:
+            @pl.when(r >= cut)
+            def _():
+                stage(t, LAGS[2] + late + rest, middle_rest)
+
         stage(t, lag, relay)
-        stage(t, lag + jnp.where(r == 0, 1, 0), last)
-
-    loop(chunks + LAGS[2] + rows + 1, pipeline)
+        if cut < rows:
+            @pl.when(r >= cut)
+            def _():
+                stage(t, lag + rest, relay_rest)
+
+        stage(t, lag + jnp.where(r == 0, 1, 0) + rest, last)
+
+    loop(chunks + LAGS[2] + rows + 1 + PAUSE, pipeline)
     loop(chunks, settle)
 
 
@@ -507,7 +535,7 @@
             collective_id=0, has_side_effects=True, vmem_limit_bytes=67043328
         ),
     )(low_t[0], inv_first[0], coupling_num[0])
-    return solved[None], swapped[None]
+    return -solved[None], -swapped[None]
 
 
 def solution(mesh):

time: 230 us -> 224 us (0.974)
  Pallas kernels: 225 us -> 219 us
  local copies, waits for them, and re-layouts: 3.92 us -> 0 us
  other arithmetic: 0 us -> 3.75 us
    pallas_call x1, Pallas kernels: 225 us -> 219 us  [local(): pl.pallas_call(functools.partial(kernel, rows, cols), out_shape=(result,...]
    unnamed x4 -> x0, local copies, waits for them, and re-layouts: 3.92 us -> none
    neg x0 -> x1, other arithmetic: none -> 3.75 us  [local(): return (-solved[None], -swapped[None])]
where the time goes in v2:
time: 224 us
  Pallas kernels  219 us (98%)
  other arithmetic  3.75 us (2%)
    pallas_call x1, Pallas kernels, local(): pl.pallas_call(functools.partial(kernel, rows, cols), out_shape=(result,...  219 us

profile of v2, /device:TPU:0, one launch (start us, length us, event | category | flops | bytes accessed | tf_op | source)
XLA Modules:
  0.0 223.7 jit_solution(15528173102884721311)
XLA Ops:
  0.6 219.4 %shard_map.50 = (f32[512,768]{1,0:T(8,128)}, f32[512,768]{1,0:T(8,128)}) custom-call(f32[512,768]{1,0:T(8,128)} %bitcast.9, f32[512,4096]{1,0:T(8,128)} %bitcast.7, s32[512,4096]{1,0:T(8,128)} %bitcast.8), custom_call_target="tpu_custom_call" | custom-call | tf_op jit(solution)/shard_map/pallas_call | solution.py:501
  220.0 3.7 %negate_bitcast_fusion = (f32[1,512,768]{2,1,0:T(8,128)}, f32[1,512,768]{2,1,0:T(8,128)}) fusion(f32[512,768]{1,0:T(8,128)} %get-tuple-element.5, f32[512,768]{1,0:T(8,128)} %get-tuple-element.4), kind=kLoop, calls=%fused_computation | loop fusion | flops 786432 | bytes 6291456 | tf_op jit(solution)/shard_map/neg | solution.py:538

commit v3 on v2

--- a/solution.py
+++ b/solution.py
@@ -319,6 +319,11 @@
         own[n, r] = acc[...]
         form(1, n, acc[...], 0, cut)
 
+        @pl.when((r == final) & (r > 0) & ~direct(n))
+        def _():
+            for d in range(1, cols):
+                far_copy(n, d).start()
+
     def middle_rest(n):
         form(1, n, own[n, r], cut, rows)
 
@@ -334,7 +339,7 @@
                 far_copy(n, d).wait_recv()
                 sendb[n, d - 1, 0] += hop_in[n, rows - 2 + d]
 
-        @pl.when(below & ~direct(n))
+        @pl.when(below & (r < final))
         def _():
             for d in range(1, cols):
                 far_copy(n, d).start()

time: 224 us -> 224 us (level)
  no operation moved by 1% of the time
where the time goes in v3:
time: 224 us
  Pallas kernels  219 us (98%)
  other arithmetic  3.75 us (2%)
    pallas_call x1, Pallas kernels, local(): pl.pallas_call(functools.partial(kernel, rows, cols), out_shape=(result,...  219 us

profile of v3, /device:TPU:0, one launch (start us, length us, event | category | flops | bytes accessed | tf_op | source)
XLA Modules:
  0.0 223.5 jit_solution(6489376135635866634)
XLA Ops:
  0.6 219.1 %shard_map.50 = (f32[512,768]{1,0:T(8,128)}, f32[512,768]{1,0:T(8,128)}) custom-call(f32[512,768]{1,0:T(8,128)} %bitcast.9, f32[512,4096]{1,0:T(8,128)} %bitcast.7, s32[512,4096]{1,0:T(8,128)} %bitcast.8), custom_call_target="tpu_custom_call" | custom-call | tf_op jit(solution)/shard_map/pallas_call | solution.py:506
  219.8 3.7 %negate_bitcast_fusion = (f32[1,512,768]{2,1,0:T(8,128)}, f32[1,512,768]{2,1,0:T(8,128)}) fusion(f32[512,768]{1,0:T(8,128)} %get-tuple-element.5, f32[512,768]{1,0:T(8,128)} %get-tuple-element.4), kind=kLoop, calls=%fused_computation | loop fusion | flops 786432 | bytes 6291456 | tf_op jit(solution)/shard_map/neg | solution.py:543
